TPU v7x, 128 devices: a whole 4x4x4 slice. The times are simulated.
128 devices in a mesh: row: 8 (over z, core), col: 16 (over x, y).
Axes of the slice: x: 4, y: 4, z: 4, core: 2. Of those that a mesh axis runs over, the one named last changes fastest.
Arguments:
- embed: bfloat16 [262144, 64], P(('row', 'col')), may hold values from -6 to 6
- tiles: bfloat16 [8192, 128, 128], P(('row', 'col'))
- tile_rows: int32 [8192], P(('row', 'col')), may hold values from 0 to 2047, as said below
- tile_cols: int32 [8192], P(('row', 'col')), may hold values from 0 to 2047, as said below
- chg_tiles: bfloat16 [24576, 128, 128], P(('row', 'col'))
- chg_rows: int32 [24576], P(('row', 'col')), may hold values from 0 to 2047, as said below
- chg_cols: int32 [24576], P(('row', 'col')), may hold values from 0 to 2047, as said below
Outputs:
- embedding: float32 [262144, 64], P(('row', 'col'))
Inputs may be any that keep to these rules, and one draw needn't show every extreme that they name: Tile n lies in the row group of the device that holds it: tile_rows[n] // 256 equals (n // 64) // 16. Tile n lies in the column group of the device that holds it: tile_cols[n] // 128 equals (n // 64) % 16. `chg_rows`: one device's list names each transpose owner at most 3 times; in every draw some owner is named exactly 3 times by every device's list. `chg_cols`: read with chg_rows to give the transpose owner.
All inputs are finite; a program needn't handle non-finite values.
Results may differ from a plain program's by a relative error of at most 0.025.
Values may be sent and summed in bfloat16 or wider, within the bound.
A program may use at most 192 MiB of HBM per device.

v0:
```python
import jax
import jax.numpy as jnp
from jax import lax
from jax.sharding import PartitionSpec as P

ITERS = 3
CAP = 3


def block_terms(own, own_rows, own_cols, taken, taken_rows, taken_cols, blocked, row_blocks):
    own_terms = jnp.einsum(
        "nab,nbk->nak", own, blocked[own_cols], preferred_element_type=jnp.float32
    )
    taken_terms = jnp.einsum(
        "nab,nak->nbk", taken, blocked[taken_cols], preferred_element_type=jnp.float32
    )
    return jax.ops.segment_sum(own_terms, own_rows, row_blocks) + jax.ops.segment_sum(
        taken_terms, taken_rows, row_blocks
    )


def local(embed, tiles, tile_rows, tile_cols, chg_tiles, chg_rows, chg_cols):
    rows_dev, feature_width = embed.shape
    tile_size = tiles.shape[1]
    row_count = lax.axis_size("row")
    col_count = lax.axis_size("col")
    devices = row_count * col_count
    row_blocks = rows_dev * col_count // tile_size
    col_blocks = rows_dev * row_count // tile_size
    sub_rows = rows_dev // devices
    owners = chg_cols // row_blocks * col_count + chg_rows // col_blocks
    position = jnp.arange(owners.shape[0], dtype=jnp.int32)
    earlier = position[None, :] < position[:, None]
    slot_rank = jnp.sum(jnp.logical_and(owners[:, None] == owners[None, :], earlier), axis=1)
    outgoing = (
        jnp.zeros((devices, CAP, tile_size, tile_size), jnp.bfloat16)
        .at[owners, slot_rank]
        .set(chg_tiles)
    )
    placing = jnp.stack([chg_cols % row_blocks, chg_rows % col_blocks], axis=1)
    output_slots = jnp.zeros((devices, CAP, 2), jnp.int32).at[owners, slot_rank].set(placing)
    taken, taken_places = (
        lax.all_to_all(outgoing, ("row", "col"), split_axis=0, concat_axis=0, tiled=True),
        lax.all_to_all(output_slots, ("row", "col"), split_axis=0, concat_axis=0, tiled=True),
    )
    taken = taken.reshape(devices * CAP, tile_size, tile_size)
    taken_places = taken_places.reshape(devices * CAP, 2)
    taken_rows = taken_places[:, 0]
    taken_cols = taken_places[:, 1]
    own_rows = tile_rows % row_blocks
    own_cols = tile_cols % col_blocks
    degree_terms = jax.ops.segment_sum(
        jnp.sum(jnp.abs(tiles), axis=2, dtype=jnp.float32), own_rows, row_blocks
    )
    degree_terms = degree_terms + jax.ops.segment_sum(
        jnp.sum(jnp.abs(taken), axis=1, dtype=jnp.float32), taken_rows, row_blocks
    )
    degree = 1.0 + lax.psum_scatter(
        degree_terms.astype(jnp.bfloat16), "col", scatter_dimension=0, tiled=True
    ).astype(jnp.float32).reshape(rows_dev, 1)
    nodes = rows_dev * devices
    current = embed
    final_output = embed.astype(jnp.float32)
    for iteration in range(ITERS):
        received_terms = lax.all_to_all(
            current.reshape(devices, sub_rows, feature_width),
            ("row", "col"),
            split_axis=0,
            concat_axis=0,
            tiled=True,
        )
        group = lax.all_gather(
            received_terms.reshape(rows_dev, feature_width), "row", axis=0, tiled=True
        )
        blocked = group.reshape(col_blocks, tile_size, feature_width)
        partial_value = block_terms(
            tiles, own_rows, own_cols, taken, taken_rows, taken_cols, blocked, row_blocks
        )
        summed = lax.psum_scatter(
            partial_value.reshape(row_blocks * tile_size, feature_width).astype(jnp.bfloat16),
            "col",
            scatter_dimension=0,
            tiled=True,
        ).astype(jnp.float32)
        scaled = summed / degree
        local_gram = jnp.dot(
            scaled.T, scaled, precision=lax.Precision.HIGHEST, preferred_element_type=jnp.float32
        )
        gram = lax.psum(local_gram, ("row", "col")) / nodes
        lower = jnp.linalg.cholesky(gram)
        final_output = lax.linalg.triangular_solve(
            lower, scaled, left_side=False, lower=True, transpose_a=True
        )
        current = final_output.astype(jnp.bfloat16)
    return final_output


def solution(mesh):
    placed = (
        P(("row", "col"), None),
        P(("row", "col"), None, None),
        P(("row", "col")),
        P(("row", "col")),
        P(("row", "col"), None, None),
        P(("row", "col")),
        P(("row", "col")),
    )
    return jax.shard_map(
        local, mesh=mesh, in_specs=placed, out_specs=P(("row", "col"), None), check_vma=False
    )
```

profile of v0, /device:TPU:1, one launch (start us, length us, event | category | flops | bytes accessed | tf_op | source)
XLA Modules:
  0.0 1204.5 jit_solution(14980614209809009102)
XLA Ops:
  8.4 10.1 scatter_fusion.1
  20.0 11.5 all-to-all-start.1
  53.4 30.8 %scatter_fusion.2 = bf16[128,3,128,128]{3,2,1,0:T(8,128)(2,1)} fusion(bf16[128,3,128,128]{3,2,1,0:T(8,128)(2,1)} %broadcast_in_dim.14, s32[192]{0:T(256)S(1)} %bitcast.91, bf16[192,128,128]{2,1,0:T(8,128)(2,1)} %param.14), kind=kCustom, calls=%fused_computation.8 | custom fusion | bytes 18875904 | tf_op jit(solution)/shard_map/scatter | solution.py:38
  84.2 10.2 all-to-all-start.2
  97.6 142.3 %all-gather.4.cloned.1.call-done = bf16[16384,64]{1,0:T(8,128)(2,1)} async-done(((bf16[2048,64]{1,0:T(8,128)(2,1)}), bf16[16384,64]{1,0:T(8,128)(2,1)}) %all-gather.4.cloned.1.call-update) | async-done | bytes 2097168 | tf_op jit(solution)/shard_map/all_gather | solution.py:72
  243.8 13.3 %gather_fusion.1 = bf16[384,128,64]{1,2,0:T(8,128)(2,1)} fusion(bf16[128,128,64]{1,2,0:T(8,128)(2,1)S(1)} %copy.77, s32[1024]{0:T(1024)S(1)} %pad_clamp_fusion), kind=kCustom, calls=%fused_computation.1 | custom fusion | bytes 12584448 | tf_op jit(solution)/shard_map/gather | solution.py:15
  265.2 9.0 scatter_fusion
  274.2 9.2 convert_reduce_fusion
  286.7 14.3 %fusion.38 = f32[384,128,64]{1,2,0:T(8,128)} fusion(bf16[384,128,64]{1,2,0:T(8,128)(2,1)} %gather_fusion.1, bf16[384,128,128]{2,1,0:T(8,128)(2,1)} %bitcast.9), kind=kOutput, calls=%fused_computation.120 | convolution fusion | flops 805306368 | bytes 31457280 | tf_op jit(solution)/shard_map/nab,nak->nbk/dot_general | solution.py:14
  305.3 59.8 %scatter_fusion.3 = f32[256,128,64]{1,2,0:T(8,128)} fusion(f32[256,128,64]{1,2,0:T(8,128)} %broadcast.110.clone.3, s32[384]{0:T(512)S(1)} %get-tuple-element.8, f32[384,128,64]{1,2,0:T(8,128)} %fusion.38), kind=kCustom, calls=%fused_computation.9 | custom fusion | flops 3145728 | bytes 37750272 | tf_op jit(solution)/shard_map/scatter-add | solution.py:17
  365.1 8.6 copy_bitcast_fusion.2
  375.0 8.3 all-reduce.3.cloned.1.call-done
  384.0 84.0 %reduce-scatter.4.cloned.1.call-done = bf16[2048,64]{0,1:T(8,128)(2,1)} async-done(((bf16[32768,64]{0,1:T(8,128)(2,1)}), bf16[2048,64]{0,1:T(8,128)(2,1)}) %reduce-scatter.4.cloned.1.call-update) | async-done | bytes 262160 | tf_op jit(solution)/shard_map/reduce_scatter | solution.py:79
  469.7 66.1 %psum.21 = f32[64,64]{0,1:T(8,128)S(1)} all-reduce(f32[64,64]{0,1:T(8,128)S(1)} %fusion.5), channel_id=1, replica_groups=mesh['row'=8,'col'=16] {'row','col'}, use_global_device_ids=true, to_apply=%region_11.12 | all-reduce | flops 4096 | bytes 32768 | tf_op jit(solution)/shard_map/psum | solution.py:89
  550.2 15.7 %all_to_all.25 = bf16[128,2,512]{2,1,0:T(2,128)(2,1)S(1)} all-to-all(bf16[128,2,512]{2,1,0:T(2,128)(2,1)S(1)} %reshape.237), channel_id=1, replica_groups=mesh['row'=8,'col'=16] {'row','col'}, dimensions={0} | all-to-all | bytes 524288 | tf_op jit(solution)/shard_map/all_to_all | solution.py:65
  567.3 28.7 %all-gather.6.cloned.1.call-done = bf16[16384,64]{1,0:T(8,128)(2,1)} async-done(((bf16[2048,64]{1,0:T(8,128)(2,1)}), bf16[16384,64]{1,0:T(8,128)(2,1)}) %all-gather.6.cloned.1.call-update) | async-done | bytes 2097168 | tf_op jit(solution)/shard_map/all_gather | solution.py:72
  599.6 13.3 %gather_fusion.3 = bf16[384,128,64]{1,2,0:T(8,128)(2,1)} fusion(bf16[128,128,64]{1,2,0:T(8,128)(2,1)S(1)} %copy.87, s32[1024]{0:T(1024)S(1)} %pad_clamp_fusion), kind=kCustom, calls=%fused_computation.3 | custom fusion | bytes 12584448 | tf_op jit(solution)/shard_map/gather | solution.py:15
  613.7 14.4 %fusion.39 = f32[384,128,64]{1,2,0:T(8,128)} fusion(bf16[384,128,64]{1,2,0:T(8,128)(2,1)} %gather_fusion.3, bf16[384,128,128]{2,1,0:T(8,128)(2,1)} %bitcast.9), kind=kOutput, calls=%fused_computation.121 | convolution fusion | flops 805306368 | bytes 31457280 | tf_op jit(solution)/shard_map/nab,nak->nbk/dot_general | solution.py:14
  633.9 59.8 %scatter_fusion.5 = f32[256,128,64]{1,2,0:T(8,128)} fusion(f32[256,128,64]{1,2,0:T(8,128)} %broadcast.110.clone.4, s32[384]{0:T(512)S(1)} %get-tuple-element.8, f32[384,128,64]{1,2,0:T(8,128)} %fusion.39), kind=kCustom, calls=%fused_computation.13 | custom fusion | flops 3145728 | bytes 37750272 | tf_op jit(solution)/shard_map/scatter-add | solution.py:17
  698.0 9.2 scatter_fusion.4
  707.2 8.6 copy_bitcast_fusion.1
  715.9 75.9 %reduce-scatter.6.cloned.1.call-done = bf16[2048,64]{0,1:T(8,128)(2,1)} async-done(((bf16[32768,64]{0,1:T(8,128)(2,1)}), bf16[2048,64]{0,1:T(8,128)(2,1)}) %reduce-scatter.6.cloned.1.call-update) | async-done | bytes 262160 | tf_op jit(solution)/shard_map/reduce_scatter | solution.py:79
  793.4 66.2 %psum.22 = f32[64,64]{0,1:T(8,128)S(1)} all-reduce(f32[64,64]{0,1:T(8,128)S(1)} %fusion.6), channel_id=1, replica_groups=mesh['row'=8,'col'=16] {'row','col'}, use_global_device_ids=true, to_apply=%region_17.20 | all-reduce | flops 4096 | bytes 32768 | tf_op jit(solution)/shard_map/psum | solution.py:89
  873.9 15.7 %all_to_all.26 = bf16[128,2,512]{2,1,0:T(2,128)(2,1)S(1)} all-to-all(bf16[128,2,512]{2,1,0:T(2,128)(2,1)S(1)} %reshape.239), channel_id=1, replica_groups=mesh['row'=8,'col'=16] {'row','col'}, dimensions={0} | all-to-all | bytes 524288 | tf_op jit(solution)/shard_map/all_to_all | solution.py:65
  890.9 28.8 %all-gather.8.cloned.1.call-done = bf16[16384,64]{1,0:T(8,128)(2,1)} async-done(((bf16[2048,64]{1,0:T(8,128)(2,1)}), bf16[16384,64]{1,0:T(8,128)(2,1)}) %all-gather.8.cloned.1.call-update) | async-done | bytes 2097168 | tf_op jit(solution)/shard_map/all_gather | solution.py:72
  923.4 13.3 %gather_fusion.5 = bf16[384,128,64]{1,2,0:T(8,128)(2,1)} fusion(bf16[128,128,64]{1,2,0:T(8,128)(2,1)S(1)} %copy.94, s32[1024]{0:T(1024)S(1)} %pad_clamp_fusion), kind=kCustom, calls=%fused_computation.5 | custom fusion | bytes 12584448 | tf_op jit(solution)/shard_map/gather | solution.py:15
  937.5 14.4 %fusion.40 = f32[384,128,64]{1,2,0:T(8,128)} fusion(bf16[384,128,64]{1,2,0:T(8,128)(2,1)} %gather_fusion.5, bf16[384,128,128]{2,1,0:T(8,128)(2,1)} %bitcast.9), kind=kOutput, calls=%fused_computation.122 | convolution fusion | flops 805306368 | bytes 31457280 | tf_op jit(solution)/shard_map/nab,nak->nbk/dot_general | solution.py:14
  957.7 58.9 %scatter_fusion.7 = f32[256,128,64]{1,2,0:T(8,128)} fusion(f32[256,128,64]{1,2,0:T(8,128)} %broadcast.110.clone.5, s32[384]{0:T(512)S(1)} %get-tuple-element.8, f32[384,128,64]{1,2,0:T(8,128)} %fusion.40), kind=kCustom, calls=%fused_computation.15 | custom fusion | flops 3145728 | bytes 37750272 | tf_op jit(solution)/shard_map/scatter-add | solution.py:17
  1020.9 9.2 scatter_fusion.6
  1030.1 8.5 copy_bitcast_fusion
  1038.7 75.5 %reduce-scatter.8.cloned.1.call-done = bf16[2048,64]{0,1:T(8,128)(2,1)} async-done(((bf16[32768,64]{0,1:T(8,128)(2,1)}), bf16[2048,64]{0,1:T(8,128)(2,1)}) %reduce-scatter.8.cloned.1.call-update) | async-done | bytes 262160 | tf_op jit(solution)/shard_map/reduce_scatter | solution.py:79
  1115.9 66.3 %psum.23 = f32[64,64]{0,1:T(8,128)S(1)} all-reduce(f32[64,64]{0,1:T(8,128)S(1)} %fusion.7), channel_id=1, replica_groups=mesh['row'=8,'col'=16] {'row','col'}, use_global_device_ids=true, to_apply=%region_21.24 | all-reduce | flops 4096 | bytes 32768 | tf_op jit(solution)/shard_map/psum | solution.py:89
  (106 shorter events, 128.1 us)
Async XLA Ops:
  20.0 21.6 %all-to-all-start.1 = ((s32[128,3,2]{1,2,0:T(2,128)}), s32[128,3,2]{1,2,0:T(2,128)S(1)}, u32[]{:S(2)}, u32[]{:S(2)}) async-start(s32[128,3,2]{1,2,0:T(2,128)} %copy.79), calls=%async_computation.1 | async-start | bytes 262144 | tf_op jit(solution)/shard_map/all_to_all | solution.py:44
  41.6 42.6 %all-to-all-start = ((bf16[128,2,512]{2,1,0:T(2,128)(2,1)}), bf16[128,2,512]{2,1,0:T(2,128)(2,1)S(1)}, u32[]{:S(2)}, u32[]{:S(2)}) async-start(bf16[128,2,512]{2,1,0:T(2,128)(2,1)} %reshape.235), calls=%async_computation | async-start | bytes 524288 | tf_op jit(solution)/shard_map/all_to_all | solution.py:65
  84.2 11.5 copy-start.3
  84.2 11.6 copy-start
  84.2 13.1 %copy-start.4 = (s32[64]{0:T(128)S(1)}, s32[64]{0:T(128)}, u32[]{:S(2)}) copy-start(s32[64]{0:T(128)} %param.13) | copy-start | bytes 772
  84.2 190.0 %all-to-all-start.2 = ((bf16[128,3,128,128]{3,2,1,0:T(8,128)(2,1)}), bf16[128,3,128,128]{3,2,1,0:T(8,128)(2,1)}, u32[]{:S(2)}, u32[]{:S(2)}) async-start(bf16[128,3,128,128]{3,2,1,0:T(8,128)(2,1)} %scatter_fusion.2), calls=%async_computation.2 | async-start | bytes 25165824 | tf_op jit(solution)/shard_map/all_to_all | solution.py:43
  94.5 145.4 %all-gather.4.cloned.1.call-start = ((), (), s32[]{:S(2)}) async-start(), calls=%async_computation.8 | async-start | bytes 4718592 | tf_op jit(solution)/shard_map/all_gather | solution.py:72
  95.7 287.6 %all-reduce.3.cloned.1.call-start = ((), (), s32[]{:S(2)}) async-start(), calls=%async_computation.14 | async-start | bytes 131072
  286.7 181.4 %reduce-scatter.4.cloned.1.call-start = ((), (), s32[]{:S(2)}) async-start(), calls=%async_computation.9 | async-start | bytes 4456448 | tf_op jit(solution)/shard_map/reduce_scatter | solution.py:79
  365.1 8.7 copy-start.5
  373.7 222.2 %all-gather.6.cloned.1.call-start = ((), (), s32[]{:S(2)}) async-start(), calls=%async_computation.10 | async-start | bytes 4718592 | tf_op jit(solution)/shard_map/all_gather | solution.py:72
  567.1 224.7 %reduce-scatter.6.cloned.1.call-start = ((), (), s32[]{:S(2)}) async-start(), calls=%async_computation.11 | async-start | bytes 4456448 | tf_op jit(solution)/shard_map/reduce_scatter | solution.py:79
  613.7 14.4 %copy-start.1 = (bf16[64,128,128]{2,1,0:T(8,128)(2,1)S(1)}, bf16[64,128,128]{2,1,0:T(8,128)(2,1)}, u32[]{:S(2)}) copy-start(bf16[64,128,128]{2,1,0:T(8,128)(2,1)} %param.11) | copy-start | bytes 6291460
  715.8 203.9 %all-gather.8.cloned.1.call-start = ((), (), s32[]{:S(2)}) async-start(), calls=%async_computation.12 | async-start | bytes 4718592 | tf_op jit(solution)/shard_map/all_gather | solution.py:72
  890.8 223.4 %reduce-scatter.8.cloned.1.call-start = ((), (), s32[]{:S(2)}) async-start(), calls=%async_computation.13 | async-start | bytes 4456448 | tf_op jit(solution)/shard_map/reduce_scatter | solution.py:79
  937.5 14.4 %copy-start.2 = (bf16[64,128,128]{2,1,0:T(8,128)(2,1)S(1)}, bf16[64,128,128]{2,1,0:T(8,128)(2,1)}, u32[]{:S(2)}) copy-start(bf16[64,128,128]{2,1,0:T(8,128)(2,1)} %param.11) | copy-start | bytes 6291460
Sparse Core Ops, SparseCore 0:
  97.1 142.6 all-gather.3
  567.2 28.7 all-gather.5
  891.0 28.7 all-gather.7
Sparse Core Ops, SparseCore 1:
  286.7 96.5 all-reduce.2
  386.9 81.1 reduce-scatter.3
  715.9 75.8 reduce-scatter.5
  1038.8 75.4 reduce-scatter.7
where the time goes:
time: 1210 us; the launch traced here: 1200 us
  waiting for transfers between devices  451 us (37%)
  other arithmetic  283 us (23%)
  blocking collectives  230 us (19%)
  local copies, waits for them, and re-layouts  137 us (11%)
  matrix products  59.8 us (5%)
  starting transfers between devices  26.3 us (2%)
  between operations  16.4 us (1%)
    reduce_scatter x3, waiting for transfers between devices, local(): lax.psum_scatter(partial_value.reshape(row_blocks * tile_size, feature_wi...  235 us
    all_gather x3, waiting for transfers between devices, local(): lax.all_gather(received_terms.reshape(rows_dev, feature_width), 'row', ax...  200 us
    psum x3, blocking collectives, local(): gram = lax.psum(local_gram, ('row', 'col')) / nodes  199 us
    scatter-add x3, other arithmetic, block_terms(): jax.ops.segment_sum(taken_terms, taken_rows, row_blocks)  179 us
    dot_general x3, matrix products, block_terms(): jnp.einsum('nab,nak->nbk', taken, blocked[taken_cols], preferred_element_...  43.1 us
    gather x3, local copies, waits for them, and re-layouts, block_terms(): blocked[taken_cols]  39.8 us
    all_to_all x2, blocking collectives, local(): lax.all_to_all(current.reshape(devices, sub_rows, feature_width), ('row',...  31.5 us
    scatter x1, local copies, waits for them, and re-layouts, local(): outgoing = jnp.zeros((devices, CAP, tile_size, tile_size), jnp.bfloat16)....  30.8 us
  transfers between devices with their start and end apart: 10, of which 8 were waited for; matrix products, arithmetic and copies ran while one was open for 14% of the time, Pallas kernels for 0%

commit v1 on v0

--- a/solution.py
+++ b/solution.py
@@ -86,7 +86,7 @@
         local_gram = jnp.dot(
             scaled.T, scaled, precision=lax.Precision.HIGHEST, preferred_element_type=jnp.float32
         )
-        gram = lax.psum(local_gram, ("row", "col")) / nodes
+        gram = jnp.sum(lax.all_gather(local_gram, ("row", "col")), axis=0) / nodes
         lower = jnp.linalg.cholesky(gram)
         final_output = lax.linalg.triangular_solve(
             lower, scaled, left_side=False, lower=True, transpose_a=True

time: 1210 us -> 1230 us (1.017)
  waiting for transfers between devices: 451 us -> 657 us
  blocking collectives: 230 us -> 32.6 us
    all_gather x0 -> x3, waiting for transfers between devices: none -> 205 us  [local(): gram = jnp.sum(lax.all_gather(local_gram, ('row', 'col')), axis=0) / nodes]
    psum x3 -> x0, blocking collectives: 199 us -> none  [local(): gram = lax.psum(local_gram, ('row', 'col')) / nodes]
  transfers between devices with their start and end apart: 10 -> 13, of which waited for: 8 -> 11; matrix products, arithmetic and copies ran while one was open for 14% -> 14% of each run, Pallas kernels for 0% -> 0%
where the time goes in v1:
time: 1230 us; the launch traced here: 1220 us
  waiting for transfers between devices  657 us (53%)
  other arithmetic  291 us (24%)
  local copies, waits for them, and re-layouts  138 us (11%)
  matrix products  59 us (5%)
  blocking collectives  32.6 us (3%)
  starting transfers between devices  26.3 us (2%)
  between operations  16.7 us (1%)
    reduce_scatter x3, waiting for transfers between devices, local(): lax.psum_scatter(partial_value.reshape(row_blocks * tile_size, feature_wi...  235 us
    all_gather x3, waiting for transfers between devices, local(): gram = jnp.sum(lax.all_gather(local_gram, ('row', 'col')), axis=0) / nodes  205 us
    all_gather x3, waiting for transfers between devices, local(): lax.all_gather(received_terms.reshape(rows_dev, feature_width), 'row', ax...  200 us
    scatter-add x3, other arithmetic, block_terms(): jax.ops.segment_sum(taken_terms, taken_rows, row_blocks)  179 us
    dot_general x3, matrix products, block_terms(): jnp.einsum('nab,nak->nbk', taken, blocked[taken_cols], preferred_element_...  43.1 us
    gather x3, local copies, waits for them, and re-layouts, block_terms(): blocked[taken_cols]  39.8 us
    all_to_all x2, blocking collectives, local(): lax.all_to_all(current.reshape(devices, sub_rows, feature_width), ('row',...  32.6 us
    scatter x1, local copies, waits for them, and re-layouts, local(): outgoing = jnp.zeros((devices, CAP, tile_size, tile_size), jnp.bfloat16)....  30.8 us
  transfers between devices with their start and end apart: 13, of which 11 were waited for; matrix products, arithmetic and copies ran while one was open for 14% of the time, Pallas kernels for 0%

profile of v1, /device:TPU:1, one launch (start us, length us, event | category | flops | bytes accessed | tf_op | source)
XLA Modules:
  0.0 1219.7 jit_solution(14361753959178189297)
XLA Ops:
  8.4 10.1 scatter_fusion.1
  20.0 11.5 all-to-all-start.1
  53.4 30.8 %scatter_fusion.2 = bf16[128,3,128,128]{3,2,1,0:T(8,128)(2,1)} fusion(bf16[128,3,128,128]{3,2,1,0:T(8,128)(2,1)} %broadcast_in_dim.14, s32[192]{0:T(256)S(1)} %bitcast.94, bf16[192,128,128]{2,1,0:T(8,128)(2,1)} %param.14), kind=kCustom, calls=%fused_computation.8 | custom fusion | bytes 18875904 | tf_op jit(solution)/shard_map/scatter | solution.py:38
  84.2 10.2 all-to-all-start.2
  97.6 142.3 %all-gather.10.cloned.1.call-done = bf16[16384,64]{1,0:T(8,128)(2,1)} async-done(((bf16[2048,64]{1,0:T(8,128)(2,1)}), bf16[16384,64]{1,0:T(8,128)(2,1)}) %all-gather.10.cloned.1.call-update) | async-done | bytes 2097168 | tf_op jit(solution)/shard_map/all_gather | solution.py:72
  243.8 13.3 %gather_fusion.1 = bf16[384,128,64]{1,2,0:T(8,128)(2,1)} fusion(bf16[128,128,64]{1,2,0:T(8,128)(2,1)S(1)} %copy.68, s32[1024]{0:T(1024)S(1)} %pad_clamp_fusion), kind=kCustom, calls=%fused_computation.1 | custom fusion | bytes 12584448 | tf_op jit(solution)/shard_map/gather | solution.py:15
  265.2 9.0 scatter_fusion
  274.2 9.2 convert_reduce_fusion
  286.7 14.3 %fusion.38 = f32[384,128,64]{1,2,0:T(8,128)} fusion(bf16[384,128,64]{1,2,0:T(8,128)(2,1)} %gather_fusion.1, bf16[384,128,128]{2,1,0:T(8,128)(2,1)} %bitcast.9), kind=kOutput, calls=%fused_computation.120 | convolution fusion | flops 805306368 | bytes 31457280 | tf_op jit(solution)/shard_map/nab,nak->nbk/dot_general | solution.py:14
  305.3 59.8 %scatter_fusion.3 = f32[256,128,64]{1,2,0:T(8,128)} fusion(f32[256,128,64]{1,2,0:T(8,128)} %broadcast.110.clone.3, s32[384]{0:T(512)S(1)} %get-tuple-element.8, f32[384,128,64]{1,2,0:T(8,128)} %fusion.38), kind=kCustom, calls=%fused_computation.9 | custom fusion | flops 3145728 | bytes 37750272 | tf_op jit(solution)/shard_map/scatter-add | solution.py:17
  365.1 8.6 copy_bitcast_fusion.2
  375.0 8.3 all-reduce.3.cloned.1.call-done
  384.0 84.0 %reduce-scatter.4.cloned.1.call-done = bf16[2048,64]{0,1:T(8,128)(2,1)} async-done(((bf16[32768,64]{0,1:T(8,128)(2,1)}), bf16[2048,64]{0,1:T(8,128)(2,1)}) %reduce-scatter.4.cloned.1.call-update) | async-done | bytes 262160 | tf_op jit(solution)/shard_map/reduce_scatter | solution.py:79
  470.4 68.3 %all-gather.16.cloned.1.call-done = f32[8192,64]{1,0:T(8,128)} async-done(((f32[64,64]{1,0:T(8,128)}), f32[8192,64]{1,0:T(8,128)}) %all-gather.16.cloned.1.call-update) | async-done | bytes 2097168 | tf_op jit(solution)/shard_map/all_gather | solution.py:89
  554.8 16.3 %all_to_all.25 = bf16[128,2,512]{2,1,0:T(2,128)(2,1)S(1)} all-to-all(bf16[128,2,512]{2,1,0:T(2,128)(2,1)S(1)} %reshape.240), channel_id=1, replica_groups=mesh['row'=8,'col'=16] {'row','col'}, dimensions={0} | all-to-all | bytes 524288 | tf_op jit(solution)/shard_map/all_to_all | solution.py:65
  572.3 28.8 %all-gather.12.cloned.1.call-done = bf16[16384,64]{1,0:T(8,128)(2,1)} async-done(((bf16[2048,64]{1,0:T(8,128)(2,1)}), bf16[16384,64]{1,0:T(8,128)(2,1)}) %all-gather.12.cloned.1.call-update) | async-done | bytes 2097168 | tf_op jit(solution)/shard_map/all_gather | solution.py:72
  605.0 13.3 %gather_fusion.3 = bf16[384,128,64]{1,2,0:T(8,128)(2,1)} fusion(bf16[128,128,64]{1,2,0:T(8,128)(2,1)S(1)} %copy.78, s32[1024]{0:T(1024)S(1)} %pad_clamp_fusion), kind=kCustom, calls=%fused_computation.3 | custom fusion | bytes 12584448 | tf_op jit(solution)/shard_map/gather | solution.py:15
  619.1 14.4 %fusion.39 = f32[384,128,64]{1,2,0:T(8,128)} fusion(bf16[384,128,64]{1,2,0:T(8,128)(2,1)} %gather_fusion.3, bf16[384,128,128]{2,1,0:T(8,128)(2,1)} %bitcast.9), kind=kOutput, calls=%fused_computation.121 | convolution fusion | flops 805306368 | bytes 31457280 | tf_op jit(solution)/shard_map/nab,nak->nbk/dot_general | solution.py:14
  639.3 59.8 %scatter_fusion.5 = f32[256,128,64]{1,2,0:T(8,128)} fusion(f32[256,128,64]{1,2,0:T(8,128)} %broadcast.110.clone.4, s32[384]{0:T(512)S(1)} %get-tuple-element.8, f32[384,128,64]{1,2,0:T(8,128)} %fusion.39), kind=kCustom, calls=%fused_computation.13 | custom fusion | flops 3145728 | bytes 37750272 | tf_op jit(solution)/shard_map/scatter-add | solution.py:17
  703.4 9.2 scatter_fusion.4
  712.6 8.6 copy_bitcast_fusion.1
  721.2 75.8 %reduce-scatter.6.cloned.1.call-done = bf16[2048,64]{0,1:T(8,128)(2,1)} async-done(((bf16[32768,64]{0,1:T(8,128)(2,1)}), bf16[2048,64]{0,1:T(8,128)(2,1)}) %reduce-scatter.6.cloned.1.call-update) | async-done | bytes 262160 | tf_op jit(solution)/shard_map/reduce_scatter | solution.py:79
  799.5 68.4 %all-gather.18.cloned.1.call-done = f32[8192,64]{1,0:T(8,128)} async-done(((f32[64,64]{1,0:T(8,128)}), f32[8192,64]{1,0:T(8,128)}) %all-gather.18.cloned.1.call-update) | async-done | bytes 2097168 | tf_op jit(solution)/shard_map/all_gather | solution.py:89
  883.9 16.3 %all_to_all.26 = bf16[128,2,512]{2,1,0:T(2,128)(2,1)S(1)} all-to-all(bf16[128,2,512]{2,1,0:T(2,128)(2,1)S(1)} %reshape.242), channel_id=1, replica_groups=mesh['row'=8,'col'=16] {'row','col'}, dimensions={0} | all-to-all | bytes 524288 | tf_op jit(solution)/shard_map/all_to_all | solution.py:65
  901.4 28.8 %all-gather.14.cloned.1.call-done = bf16[16384,64]{1,0:T(8,128)(2,1)} async-done(((bf16[2048,64]{1,0:T(8,128)(2,1)}), bf16[16384,64]{1,0:T(8,128)(2,1)}) %all-gather.14.cloned.1.call-update) | async-done | bytes 2097168 | tf_op jit(solution)/shard_map/all_gather | solution.py:72
  933.9 13.3 %gather_fusion.5 = bf16[384,128,64]{1,2,0:T(8,128)(2,1)} fusion(bf16[128,128,64]{1,2,0:T(8,128)(2,1)S(1)} %copy.85, s32[1024]{0:T(1024)S(1)} %pad_clamp_fusion), kind=kCustom, calls=%fused_computation.5 | custom fusion | bytes 12584448 | tf_op jit(solution)/shard_map/gather | solution.py:15
  948.0 14.4 %fusion.40 = f32[384,128,64]{1,2,0:T(8,128)} fusion(bf16[384,128,64]{1,2,0:T(8,128)(2,1)} %gather_fusion.5, bf16[384,128,128]{2,1,0:T(8,128)(2,1)} %bitcast.9), kind=kOutput, calls=%fused_computation.122 | convolution fusion | flops 805306368 | bytes 31457280 | tf_op jit(solution)/shard_map/nab,nak->nbk/dot_general | solution.py:14
  968.2 58.9 %scatter_fusion.7 = f32[256,128,64]{1,2,0:T(8,128)} fusion(f32[256,128,64]{1,2,0:T(8,128)} %broadcast.110.clone.5, s32[384]{0:T(512)S(1)} %get-tuple-element.8, f32[384,128,64]{1,2,0:T(8,128)} %fusion.40), kind=kCustom, calls=%fused_computation.15 | custom fusion | flops 3145728 | bytes 37750272 | tf_op jit(solution)/shard_map/scatter-add | solution.py:17
  1031.4 9.2 scatter_fusion.6
  1040.6 8.5 copy_bitcast_fusion
  1049.2 75.4 %reduce-scatter.8.cloned.1.call-done = bf16[2048,64]{0,1:T(8,128)(2,1)} async-done(((bf16[32768,64]{0,1:T(8,128)(2,1)}), bf16[2048,64]{0,1:T(8,128)(2,1)}) %reduce-scatter.8.cloned.1.call-update) | async-done | bytes 262160 | tf_op jit(solution)/shard_map/reduce_scatter | solution.py:79
  1127.0 68.4 %all-gather.20.cloned.1.call-done = f32[8192,64]{1,0:T(8,128)} async-done(((f32[64,64]{1,0:T(8,128)}), f32[8192,64]{1,0:T(8,128)}) %all-gather.20.cloned.1.call-update) | async-done | bytes 2097168 | tf_op jit(solution)/shard_map/all_gather | solution.py:89
  (124 shorter events, 135.3 us)
Async XLA Ops:
  20.0 21.6 %all-to-all-start.1 = ((s32[128,3,2]{1,2,0:T(2,128)}), s32[128,3,2]{1,2,0:T(2,128)S(1)}, u32[]{:S(2)}, u32[]{:S(2)}) async-start(s32[128,3,2]{1,2,0:T(2,128)} %copy.70), calls=%async_computation.1 | async-start | bytes 262144 | tf_op jit(solution)/shard_map/all_to_all | solution.py:44
  41.6 42.6 %all-to-all-start = ((bf16[128,2,512]{2,1,0:T(2,128)(2,1)}), bf16[128,2,512]{2,1,0:T(2,128)(2,1)S(1)}, u32[]{:S(2)}, u32[]{:S(2)}) async-start(bf16[128,2,512]{2,1,0:T(2,128)(2,1)} %reshape.238), calls=%async_computation | async-start | bytes 524288 | tf_op jit(solution)/shard_map/all_to_all | solution.py:65
  84.2 11.5 copy-start.6
  84.2 11.6 copy-start
  84.2 13.1 %copy-start.7 = (s32[64]{0:T(128)S(1)}, s32[64]{0:T(128)}, u32[]{:S(2)}) copy-start(s32[64]{0:T(128)} %param.13) | copy-start | bytes 772
  84.2 190.0 %all-to-all-start.2 = ((bf16[128,3,128,128]{3,2,1,0:T(8,128)(2,1)}), bf16[128,3,128,128]{3,2,1,0:T(8,128)(2,1)}, u32[]{:S(2)}, u32[]{:S(2)}) async-start(bf16[128,3,128,128]{3,2,1,0:T(8,128)(2,1)} %scatter_fusion.2), calls=%async_computation.2 | async-start | bytes 25165824 | tf_op jit(solution)/shard_map/all_to_all | solution.py:43
  94.5 145.4 %all-gather.10.cloned.1.call-start = ((), (), s32[]{:S(2)}) async-start(), calls=%async_computation.8 | async-start | bytes 4718592 | tf_op jit(solution)/shard_map/all_gather | solution.py:72
  95.7 287.6 %all-reduce.3.cloned.1.call-start = ((), (), s32[]{:S(2)}) async-start(), calls=%async_computation.17 | async-start | bytes 131072
  286.7 181.4 %reduce-scatter.4.cloned.1.call-start = ((), (), s32[]{:S(2)}) async-start(), calls=%async_computation.9 | async-start | bytes 4456448 | tf_op jit(solution)/shard_map/reduce_scatter | solution.py:79
  365.1 8.7 copy-start.8
  373.7 165.1 %all-gather.16.cloned.1.call-start = ((), (), s32[]{:S(2)}) async-start(), calls=%async_computation.14 | async-start | bytes 4227072 | tf_op jit(solution)/shard_map/all_gather | solution.py:89
  468.0 85.6 %copy-start.3 = (bf16[2048,64]{0,1:T(8,128)(2,1)S(1)}, bf16[2048,64]{0,1:T(8,128)(2,1)}, u32[]{:S(2)}) copy-start(bf16[2048,64]{0,1:T(8,128)(2,1)} %reduce-scatter.4.cloned.1.call-done) | copy-start | bytes 786436
  470.4 130.8 %all-gather.12.cloned.1.call-start = ((), (), s32[]{:S(2)}) async-start(), calls=%async_computation.10 | async-start | bytes 4718592 | tf_op jit(solution)/shard_map/all_gather | solution.py:72
  572.3 224.8 %reduce-scatter.6.cloned.1.call-start = ((), (), s32[]{:S(2)}) async-start(), calls=%async_computation.11 | async-start | bytes 4456448 | tf_op jit(solution)/shard_map/reduce_scatter | solution.py:79
  619.0 14.4 %copy-start.1 = (bf16[64,128,128]{2,1,0:T(8,128)(2,1)S(1)}, bf16[64,128,128]{2,1,0:T(8,128)(2,1)}, u32[]{:S(2)}) copy-start(bf16[64,128,128]{2,1,0:T(8,128)(2,1)} %param.11) | copy-start | bytes 6291460
  721.2 146.6 %all-gather.18.cloned.1.call-start = ((), (), s32[]{:S(2)}) async-start(), calls=%async_computation.15 | async-start | bytes 4227072 | tf_op jit(solution)/shard_map/all_gather | solution.py:89
  797.1 85.6 %copy-start.4 = (bf16[2048,64]{0,1:T(8,128)(2,1)S(1)}, bf16[2048,64]{0,1:T(8,128)(2,1)}, u32[]{:S(2)}) copy-start(bf16[2048,64]{0,1:T(8,128)(2,1)} %reduce-scatter.6.cloned.1.call-done) | copy-start | bytes 786436
  799.4 130.8 %all-gather.14.cloned.1.call-start = ((), (), s32[]{:S(2)}) async-start(), calls=%async_computation.12 | async-start | bytes 4718592 | tf_op jit(solution)/shard_map/all_gather | solution.py:72
  901.3 223.3 %reduce-scatter.8.cloned.1.call-start = ((), (), s32[]{:S(2)}) async-start(), calls=%async_computation.13 | async-start | bytes 4456448 | tf_op jit(solution)/shard_map/reduce_scatter | solution.py:79
  947.9 14.4 %copy-start.2 = (bf16[64,128,128]{2,1,0:T(8,128)(2,1)S(1)}, bf16[64,128,128]{2,1,0:T(8,128)(2,1)}, u32[]{:S(2)}) copy-start(bf16[64,128,128]{2,1,0:T(8,128)(2,1)} %param.11) | copy-start | bytes 6291460
  1049.2 146.2 %all-gather.20.cloned.1.call-start = ((), (), s32[]{:S(2)}) async-start(), calls=%async_computation.16 | async-start | bytes 4227072 | tf_op jit(solution)/shard_map/all_gather | solution.py:89
  1124.6 85.6 %copy-start.5 = (bf16[2048,64]{0,1:T(8,128)(2,1)S(1)}, bf16[2048,64]{0,1:T(8,128)(2,1)}, u32[]{:S(2)}) copy-start(bf16[2048,64]{0,1:T(8,128)(2,1)} %reduce-scatter.8.cloned.1.call-done) | copy-start | bytes 786436
Sparse Core Ops, SparseCore 0:
  97.1 142.6 all-gather.9
  470.5 68.2 all-gather.15
  572.4 28.7 all-gather.11
  799.5 68.2 all-gather.17
  901.5 28.7 all-gather.13
  1127.1 68.2 all-gather.19
Sparse Core Ops, SparseCore 1:
  286.7 96.5 all-reduce.2
  386.9 81.1 reduce-scatter.3
  721.3 75.7 reduce-scatter.5
  1049.3 75.3 reduce-scatter.7
